TPU v7x, 32 devices: a whole 2x2x4 slice. The times are simulated.
32 devices in a mesh: fsdp: 2 (over x), ctx: 4 (over z), tp: 4 (over y, core).
Axes of the slice: x: 2, y: 2, z: 4, core: 2. Of those that a mesh axis runs over, the one named last changes fastest.
Arguments:
- tokens: bfloat16 [4, 2048, 2048], P('fsdp', 'ctx'), may hold values from -6 to 6
- tree_position: int32 [4, 2048], P('fsdp', 'ctx'), may hold values from 0 to 2047, as said below
- segment: int32 [4, 2048], P('fsdp', 'ctx'), may hold values from 0 to 6, as said below
- parent_table: int32 [4, 7], P('fsdp'), may hold values from 0 to 2, as said below
- norm1_gain: float32 [2048], replicated, may hold values from 0.5 to 1.5
- norm1_shift: float32 [2048], replicated, may hold values from -4 to 4
- query_weight: bfloat16 [2048, 2048], P('fsdp', 'tp'), may hold values from -0.125 to 0.125
- query_bias: float32 [2048], P('tp'), may hold values from -4 to 4
- key_weight: bfloat16 [2048, 2048], P('fsdp', 'tp'), may hold values from -0.125 to 0.125
- value_weight: bfloat16 [2048, 2048], P('fsdp', 'tp'), may hold values from -0.125 to 0.125
- value_bias: float32 [2048], P('tp'), may hold values from -0.75 to 0.75
- out_weight: bfloat16 [2048, 2048], P('tp', 'fsdp'), may hold values from -1.5 to 1.5
- out_bias: float32 [2048], replicated, may hold values from -4 to 4
- norm2_gain: float32 [2048], replicated, may hold values from 0.5 to 1.5
- norm2_shift: float32 [2048], replicated, may hold values from -4 to 4
- up_weight: bfloat16 [2048, 8192], P('fsdp', 'tp'), may hold values from -0.125 to 0.125
- up_bias: float32 [8192], P('tp'), may hold values from -4 to 4
- down_weight: bfloat16 [8192, 2048], P('tp', 'fsdp'), may hold values from -0.0625 to 0.0625
- down_bias: float32 [2048], replicated, may hold values from -4 to 4
- cotangent: bfloat16 [4, 2048, 2048], P('fsdp', 'ctx'), may hold values from -6 to 6
Outputs:
- layer_out: bfloat16 [4, 2048, 2048], P('fsdp', 'ctx')
- grad_tokens: bfloat16 [4, 2048, 2048], P('fsdp', 'ctx')
- grad_norm1_gain: float32 [2048], P(('fsdp', 'ctx'))
- grad_norm1_shift: float32 [2048], P(('fsdp', 'ctx'))
- grad_query_weight: float32 [2048, 2048], P(('fsdp', 'ctx'), 'tp')
- grad_query_bias: float32 [2048], P('tp')
- grad_key_weight: float32 [2048, 2048], P(('fsdp', 'ctx'), 'tp')
- grad_value_weight: float32 [2048, 2048], P(('fsdp', 'ctx'), 'tp')
- grad_value_bias: float32 [2048], P('tp')
- grad_out_weight: float32 [2048, 2048], P('tp', ('fsdp', 'ctx'))
- grad_out_bias: float32 [2048], P(('fsdp', 'ctx'))
- grad_norm2_gain: float32 [2048], P(('fsdp', 'ctx'))
- grad_norm2_shift: float32 [2048], P(('fsdp', 'ctx'))
- grad_up_weight: float32 [2048, 8192], P(('fsdp', 'ctx'), 'tp')
- grad_up_bias: float32 [8192], P('tp')
- grad_down_weight: float32 [8192, 2048], P('tp', ('fsdp', 'ctx'))
- grad_down_bias: float32 [2048], P(('fsdp', 'ctx'))
Inputs may be any that keep to these rules, and one draw needn't show every extreme that they name: `tree_position`: within each tree the rows hold the positions 0 to 2047 once each; every aligned run of 64 rows holds 64 consecutive positions in increasing order. `segment`: along increasing positions a tree runs through segments 0 to 6 in order, each nonempty and contiguous: the trunk 0 with 1024 positions, branches 1 and 2 with 512 together, leaves 3 to 6 with 512 together. `parent_table`: entry s of a tree's row is the parent of segment s: 0 for segments 0, 1 and 2; 1 for leaf 3; 2 for leaf 6; 1 or 2 for leaves 4 and 5.
All inputs are finite; a program needn't handle non-finite values.
Results may differ from a plain program's by a relative error of at most 0.024.
Values may be sent and summed in bfloat16 or wider, within the bound.
No kernel may reach another device: no remote copies, remote signals or barrier semaphores. Data moves between devices by JAX's collectives and lax.ppermute only.
A program may use at most 256 MiB of HBM per device.

v0:
```python
from functools import partial
import math
import jax
import jax.numpy as jnp
from jax import lax
from jax.sharding import PartitionSpec as P

HD = 128
NEGATIVE = -1000000000.0


def norm_rows(values, gain, shift):
    centre = jnp.mean(values, axis=-1, keepdims=True)
    centred = values - centre
    spread = jnp.mean(centred * centred, axis=-1, keepdims=True)
    return centred * lax.rsqrt(spread + 1e-05) * gain + shift


def on_path(query_pos, query_seg, key_pos, key_seg, parent):
    labels = jnp.arange(parent.shape[0], dtype=jnp.int32)
    first = jnp.sum(jnp.where(query_seg[:, None] == labels[None, :], parent[None, :], 0), axis=1)
    second = jnp.sum(jnp.where(first[:, None] == labels[None, :], parent[None, :], 0), axis=1)
    along = (
        (key_seg[None, :] == query_seg[:, None])
        | (key_seg[None, :] == first[:, None])
        | (key_seg[None, :] == second[:, None])
    )
    return along & (key_pos[None, :] <= query_pos[:, None])


def inner_rows(left, right):
    return lax.dot_general(
        left, right, (((0,), (0,)), ((), ())), preferred_element_type=jnp.float32
    )


def times_transposed(left, right):
    return lax.dot_general(
        left, right, (((1,), (1,)), ((), ())), preferred_element_type=jnp.float32
    )


def per_device(
    tokens,
    tree_position,
    segment,
    parent_table,
    norm1_gain,
    norm1_shift,
    query_weight,
    query_bias,
    key_weight,
    value_weight,
    value_bias,
    out_weight,
    out_bias,
    norm2_gain,
    norm2_shift,
    up_weight,
    up_bias,
    down_weight,
    down_bias,
    cotangent,
):
    w_query, w_key, w_value, w_out, w_up, w_down = (
        lax.all_gather(query_weight, "fsdp", axis=0, tiled=True),
        lax.all_gather(key_weight, "fsdp", axis=0, tiled=True),
        lax.all_gather(value_weight, "fsdp", axis=0, tiled=True),
        lax.all_gather(out_weight, "fsdp", axis=1, tiled=True),
        lax.all_gather(up_weight, "fsdp", axis=0, tiled=True),
        lax.all_gather(down_weight, "fsdp", axis=1, tiled=True),
    )
    key_position, key_segment = (
        lax.all_gather(tree_position, "ctx", axis=1, tiled=True),
        lax.all_gather(segment, "ctx", axis=1, tiled=True),
    )
    local_width = w_query.shape[1]
    head_count = local_width // HD
    score_scale = 1.0 / math.sqrt(HD)
    gelu_exact = partial(jax.nn.gelu, approximate=False)
    layer_rows = []
    input_grads = []
    running = [
        jnp.zeros(w_query.shape, jnp.float32),
        jnp.zeros(w_key.shape, jnp.float32),
        jnp.zeros(w_value.shape, jnp.float32),
        jnp.zeros(w_out.shape, jnp.float32),
        jnp.zeros(w_up.shape, jnp.float32),
        jnp.zeros(w_down.shape, jnp.float32),
        jnp.zeros(norm1_gain.shape, jnp.float32),
        jnp.zeros(norm1_shift.shape, jnp.float32),
        jnp.zeros(norm2_gain.shape, jnp.float32),
        jnp.zeros(norm2_shift.shape, jnp.float32),
        jnp.zeros(out_bias.shape, jnp.float32),
        jnp.zeros(down_bias.shape, jnp.float32),
    ]
    head_sums = [
        jnp.zeros(query_bias.shape, jnp.float32),
        jnp.zeros(value_bias.shape, jnp.float32),
        jnp.zeros(up_bias.shape, jnp.float32),
    ]
    for batch_index in range(tokens.shape[0]):
        inputs = tokens[batch_index].astype(jnp.float32)
        local_rows = inputs.shape[0]
        normed = norm_rows(inputs, norm1_gain, norm1_shift).astype(jnp.bfloat16)
        queries = (
            jnp.dot(normed, w_query, preferred_element_type=jnp.float32) + query_bias
        ).astype(jnp.bfloat16)
        keys_local = jnp.dot(normed, w_key, preferred_element_type=jnp.float32).astype(jnp.bfloat16)
        values_local = (
            jnp.dot(normed, w_value, preferred_element_type=jnp.float32) + value_bias
        ).astype(jnp.bfloat16)
        keys_tree, values_tree = (
            lax.all_gather(keys_local, "ctx", axis=0, tiled=True),
            lax.all_gather(values_local, "ctx", axis=0, tiled=True),
        )
        tree_rows = keys_tree.shape[0]
        visible = on_path(
            tree_position[batch_index],
            segment[batch_index],
            key_position[batch_index],
            key_segment[batch_index],
            parent_table[batch_index],
        )
        query_heads = queries.reshape(local_rows, head_count, HD)
        key_heads = keys_tree.reshape(tree_rows, head_count, HD)
        value_heads = values_tree.reshape(tree_rows, head_count, HD)
        scores = (
            jnp.einsum("qhd,khd->hqk", query_heads, key_heads, preferred_element_type=jnp.float32)
            * score_scale
        )
        scores = jnp.where(visible[None], scores, NEGATIVE)
        row_max = jnp.max(scores, axis=-1, keepdims=True)
        shifted = jnp.exp(scores - row_max)
        row_total = jnp.sum(shifted, axis=-1, keepdims=True)
        log_total = row_max + jnp.log(row_total)
        soft_low = (shifted / row_total).astype(jnp.bfloat16)
        attended = (
            jnp.einsum("hqk,khd->qhd", soft_low, value_heads, preferred_element_type=jnp.float32)
            .reshape(local_rows, local_width)
            .astype(jnp.bfloat16)
        )
        middle = inputs + (
            lax.psum(
                jnp.dot(attended, w_out, preferred_element_type=jnp.float32).astype(jnp.bfloat16),
                "tp",
            ).astype(jnp.float32)
            + out_bias
        )
        normed_mid = norm_rows(middle, norm2_gain, norm2_shift).astype(jnp.bfloat16)
        hidden = jnp.dot(normed_mid, w_up, preferred_element_type=jnp.float32) + up_bias
        active = gelu_exact(hidden).astype(jnp.bfloat16)
        result = middle + (
            lax.psum(
                jnp.dot(active, w_down, preferred_element_type=jnp.float32).astype(jnp.bfloat16),
                "tp",
            ).astype(jnp.float32)
            + down_bias
        )
        layer_rows.append(result.astype(jnp.bfloat16))
        grad_out = cotangent[batch_index]
        grad_float = grad_out.astype(jnp.float32)
        down_bias_term = jnp.sum(grad_float, axis=0)
        down_term = inner_rows(active, grad_out)
        _, gelu_pull = jax.vjp(gelu_exact, hidden)
        grad_hidden = gelu_pull(times_transposed(grad_out, w_down))[0].astype(jnp.bfloat16)
        up_bias_term = jnp.sum(grad_hidden.astype(jnp.float32), axis=0)
        up_term = inner_rows(normed_mid, grad_hidden)
        grad_normed_mid = lax.psum(
            times_transposed(grad_hidden, w_up).astype(jnp.bfloat16), "tp"
        ).astype(jnp.float32)
        _, second_pull = jax.vjp(norm_rows, middle, norm2_gain, norm2_shift)
        grad_mid_norm, second_gain_term, second_shift_term = second_pull(grad_normed_mid)
        grad_middle = grad_float + grad_mid_norm
        grad_branch = grad_middle.astype(jnp.bfloat16)
        out_bias_term = jnp.sum(grad_branch.astype(jnp.float32), axis=0)
        out_term = inner_rows(attended, grad_branch)
        grad_attended = times_transposed(grad_branch, w_out).astype(jnp.bfloat16)
        grad_heads = grad_attended.reshape(local_rows, head_count, HD)
        again = (
            jnp.einsum("qhd,khd->hqk", query_heads, key_heads, preferred_element_type=jnp.float32)
            * score_scale
        )
        again = jnp.where(visible[None], again, NEGATIVE)
        soft = jnp.exp(again - log_total)
        soft_again = soft.astype(jnp.bfloat16)
        grad_soft = jnp.einsum(
            "qhd,khd->hqk", grad_heads, value_heads, preferred_element_type=jnp.float32
        )
        inner = jnp.sum(soft * grad_soft, axis=-1, keepdims=True)
        grad_scores = (soft * (grad_soft - inner)).astype(jnp.bfloat16)
        grad_queries = (
            (
                jnp.einsum(
                    "hqk,khd->qhd", grad_scores, key_heads, preferred_element_type=jnp.float32
                )
                * score_scale
            )
            .reshape(local_rows, local_width)
            .astype(jnp.bfloat16)
        )
        key_part = (
            jnp.einsum("hqk,qhd->khd", grad_scores, query_heads, preferred_element_type=jnp.float32)
            * score_scale
        ).reshape(tree_rows, local_width)
        value_part = jnp.einsum(
            "hqk,qhd->khd", soft_again, grad_heads, preferred_element_type=jnp.float32
        ).reshape(tree_rows, local_width)
        grad_keys, grad_values = (
            lax.psum_scatter(
                key_part.astype(jnp.bfloat16), "ctx", scatter_dimension=0, tiled=True
            ).astype(jnp.float32),
            lax.psum_scatter(
                value_part.astype(jnp.bfloat16), "ctx", scatter_dimension=0, tiled=True
            ).astype(jnp.float32),
        )
        grad_keys = grad_keys.astype(jnp.bfloat16)
        grad_values = grad_values.astype(jnp.bfloat16)
        query_bias_term = jnp.sum(grad_queries.astype(jnp.float32), axis=0)
        value_bias_term = jnp.sum(grad_values.astype(jnp.float32), axis=0)
        query_term = inner_rows(normed, grad_queries)
        key_term = inner_rows(normed, grad_keys)
        value_term = inner_rows(normed, grad_values)
        grad_normed = lax.psum(
            (
                times_transposed(grad_queries, w_query)
                + times_transposed(grad_keys, w_key)
                + times_transposed(grad_values, w_value)
            ).astype(jnp.bfloat16),
            "tp",
        ).astype(jnp.float32)
        _, first_pull = jax.vjp(norm_rows, inputs, norm1_gain, norm1_shift)
        grad_in_norm, first_gain_term, first_shift_term = first_pull(grad_normed)
        input_grads.append((grad_middle + grad_in_norm).astype(jnp.bfloat16))
        head_sums = [
            head_sums[0] + query_bias_term,
            head_sums[1] + value_bias_term,
            head_sums[2] + up_bias_term,
        ]
        fresh = [
            query_term,
            key_term,
            value_term,
            out_term,
            up_term,
            down_term,
            first_gain_term,
            first_shift_term,
            second_gain_term,
            second_shift_term,
            out_bias_term,
            down_bias_term,
        ]
        running = [older + newer for older, newer in zip(running, fresh)]
    final = (
        lax.psum_scatter(
            running[0].astype(jnp.bfloat16), ("fsdp", "ctx"), scatter_dimension=0, tiled=True
        ).astype(jnp.float32),
        lax.psum_scatter(
            running[1].astype(jnp.bfloat16), ("fsdp", "ctx"), scatter_dimension=0, tiled=True
        ).astype(jnp.float32),
        lax.psum_scatter(
            running[2].astype(jnp.bfloat16), ("fsdp", "ctx"), scatter_dimension=0, tiled=True
        ).astype(jnp.float32),
        lax.psum_scatter(
            running[3].astype(jnp.bfloat16), ("fsdp", "ctx"), scatter_dimension=1, tiled=True
        ).astype(jnp.float32),
        lax.psum_scatter(
            running[4].astype(jnp.bfloat16), ("fsdp", "ctx"), scatter_dimension=0, tiled=True
        ).astype(jnp.float32),
        lax.psum_scatter(
            running[5].astype(jnp.bfloat16), ("fsdp", "ctx"), scatter_dimension=1, tiled=True
        ).astype(jnp.float32),
        lax.psum_scatter(
            running[6].astype(jnp.bfloat16), ("fsdp", "ctx"), scatter_dimension=0, tiled=True
        ).astype(jnp.float32),
        lax.psum_scatter(
            running[7].astype(jnp.bfloat16), ("fsdp", "ctx"), scatter_dimension=0, tiled=True
        ).astype(jnp.float32),
        lax.psum_scatter(
            running[8].astype(jnp.bfloat16), ("fsdp", "ctx"), scatter_dimension=0, tiled=True
        ).astype(jnp.float32),
        lax.psum_scatter(
            running[9].astype(jnp.bfloat16), ("fsdp", "ctx"), scatter_dimension=0, tiled=True
        ).astype(jnp.float32),
        lax.psum_scatter(
            running[10].astype(jnp.bfloat16), ("fsdp", "ctx"), scatter_dimension=0, tiled=True
        ).astype(jnp.float32),
        lax.psum_scatter(
            running[11].astype(jnp.bfloat16), ("fsdp", "ctx"), scatter_dimension=0, tiled=True
        ).astype(jnp.float32),
    )
    bias_totals = lax.psum((head_sums[0], head_sums[1], head_sums[2]), ("fsdp", "ctx"))
    return (
        jnp.stack(layer_rows),
        jnp.stack(input_grads),
        final[6],
        final[7],
        final[0],
        bias_totals[0],
        final[1],
        final[2],
        bias_totals[1],
        final[3],
        final[10],
        final[8],
        final[9],
        final[4],
        bias_totals[2],
        final[5],
        final[11],
    )


def solution(mesh):
    in_specs = (
        P("fsdp", "ctx", None),
        P("fsdp", "ctx"),
        P("fsdp", "ctx"),
        P("fsdp", None),
        P(),
        P(),
        P("fsdp", "tp"),
        P("tp"),
        P("fsdp", "tp"),
        P("fsdp", "tp"),
        P("tp"),
        P("tp", "fsdp"),
        P(),
        P(),
        P(),
        P("fsdp", "tp"),
        P("tp"),
        P("tp", "fsdp"),
        P(),
        P("fsdp", "ctx", None),
    )
    out_specs = (
        P("fsdp", "ctx", None),
        P("fsdp", "ctx", None),
        P(("fsdp", "ctx")),
        P(("fsdp", "ctx")),
        P(("fsdp", "ctx"), "tp"),
        P("tp"),
        P(("fsdp", "ctx"), "tp"),
        P(("fsdp", "ctx"), "tp"),
        P("tp"),
        P("tp", ("fsdp", "ctx")),
        P(("fsdp", "ctx")),
        P(("fsdp", "ctx")),
        P(("fsdp", "ctx")),
        P(("fsdp", "ctx"), "tp"),
        P("tp"),
        P("tp", ("fsdp", "ctx")),
        P(("fsdp", "ctx")),
    )
    return jax.shard_map(
        per_device, mesh=mesh, in_specs=in_specs, out_specs=out_specs, check_vma=False
    )
```

profile of v0, /device:TPU:0, one launch (start us, length us, event | category | flops | bytes accessed | tf_op | source)
XLA Modules:
  0.0 1765.6 jit_solution(16813001893812341595)
XLA Ops:
  14.5 30.9 %all-gather.17.cloned.1.call-done = bf16[2048,512]{1,0:T(8,128)(2,1)} async-done(((bf16[1024,512]{1,0:T(8,128)(2,1)}), bf16[2048,512]{1,0:T(8,128)(2,1)}) %all-gather.17.cloned.1.call-update) | async-done | bytes 2097168 | tf_op jit(solution)/shard_map/all_gather | solution.py:67
  49.2 30.9 %all-gather.11.cloned.1.call-done = bf16[2048,512]{1,0:T(8,128)(2,1)} async-done(((bf16[1024,512]{1,0:T(8,128)(2,1)}), bf16[2048,512]{1,0:T(8,128)(2,1)}) %all-gather.11.cloned.1.call-update) | async-done | bytes 2097168 | tf_op jit(solution)/shard_map/all_gather | solution.py:68
  84.4 13.3 all_gather.39
  97.6 13.4 all_gather.38
  118.4 44.0 %all-gather.19.cloned.1.call-done = bf16[2048,512]{1,0:T(8,128)(2,1)} async-done(((bf16[512,512]{1,0:T(8,128)(2,1)}), bf16[2048,512]{1,0:T(8,128)(2,1)}) %all-gather.19.cloned.1.call-update) | async-done | bytes 2097168 | tf_op jit(solution)/shard_map/all_gather | solution.py:114
  165.4 9.3 fusion.162
  174.7 8.2 fusion
  182.8 26.1 %all-gather.13.cloned.1.call-done = bf16[2048,512]{1,0:T(8,128)(2,1)} async-done(((bf16[512,512]{1,0:T(8,128)(2,1)}), bf16[2048,512]{1,0:T(8,128)(2,1)}) %all-gather.13.cloned.1.call-update) | async-done | bytes 2097168 | tf_op jit(solution)/shard_map/all_gather | solution.py:115
  208.9 8.5 fusion.127
  217.4 24.8 %all-gather.21.cloned.1.call-done = bf16[512,2048]{1,0:T(8,128)(2,1)} async-done(((bf16[512,1024]{1,0:T(8,128)(2,1)}), bf16[512,2048]{1,0:T(8,128)(2,1)}) %all-gather.21.cloned.1.call-update) | async-done | bytes 2097168 | tf_op jit(solution)/shard_map/all_gather | solution.py:69
  242.3 4.2 convolution_convert_fusion.5
  246.9 51.0 %all-reduce.15.cloned.1.call-done = bf16[512,2048]{1,0:T(8,128)(2,1)} async-done(((bf16[512,2048]{1,0:T(8,128)(2,1)}), bf16[512,2048]{1,0:T(8,128)(2,1)}) %all-reduce.15.cloned.1.call-update) | async-done | bytes 2097168 | tf_op jit(solution)/shard_map/psum | solution.py:144
  298.0 4.3 fusion.69
  312.4 4.8 fusion.123
  317.3 35.4 %all-gather.29.cloned.1.call-done = bf16[2048,512]{1,0:T(8,128)(2,1)} async-done(((bf16[512,512]{1,0:T(8,128)(2,1)}), bf16[2048,512]{1,0:T(8,128)(2,1)}) %all-gather.29.cloned.1.call-update) | async-done | bytes 2097168 | tf_op jit(solution)/shard_map/all_gather | solution.py:114
  355.6 9.5 fusion.163
  365.0 8.2 fusion.1
  373.2 26.0 %all-gather.27.cloned.1.call-done = bf16[2048,512]{1,0:T(8,128)(2,1)} async-done(((bf16[512,512]{1,0:T(8,128)(2,1)}), bf16[2048,512]{1,0:T(8,128)(2,1)}) %all-gather.27.cloned.1.call-update) | async-done | bytes 2097168 | tf_op jit(solution)/shard_map/all_gather | solution.py:115
  399.3 8.3 fusion.124
  412.6 48.8 %all-reduce.17.cloned.1.call-done = bf16[512,2048]{1,0:T(8,128)(2,1)} async-done(((bf16[512,2048]{1,0:T(8,128)(2,1)}), bf16[512,2048]{1,0:T(8,128)(2,1)}) %all-reduce.17.cloned.1.call-update) | async-done | bytes 2097168 | tf_op jit(solution)/shard_map/psum | solution.py:144
  461.4 4.5 multiply_reduce_fusion.3
  467.8 99.3 %all-gather.23.cloned.1.call-done = bf16[2048,2048]{1,0:T(8,128)(2,1)} async-done(((bf16[1024,2048]{1,0:T(8,128)(2,1)}), bf16[2048,2048]{1,0:T(8,128)(2,1)}) %all-gather.23.cloned.1.call-update) | async-done | bytes 8388624 | tf_op jit(solution)/shard_map/all_gather | solution.py:70
  567.1 8.0 fusion.142
  577.3 26.2 %multiply_convert_fusion.5 = (bf16[512,2048]{1,0:T(8,128)(2,1)}, f32[512,2048]{1,0:T(8,128)}, bf16[512,2048]{1,0:T(8,128)(2,1)}, f32[512,2048]{1,0:T(8,128)}, f32[512,2048]{1,0:T(8,128)}) fusion(f32[2048]{0:T(1024)S(1)} %copy-done.101, f32[512,2048]{1,0:T(8,128)S(1)} %fusion.142, bf16[2048,2048]{1,0:T(8,128)(2,1)S(1)} %copy-done.99, ...), kind=kOutput, calls=%fused_computation.131 | convolution fusion | flops 4442816512 | bytes 33591296 | tf_op jit(solution)/shard_map/dot_general | solution.py:151
  603.5 68.9 %all-gather.25.cloned.1.call-done = bf16[2048,2048]{1,0:T(8,128)(2,1)} async-done(((bf16[2048,1024]{1,0:T(8,128)(2,1)}), bf16[2048,2048]{1,0:T(8,128)(2,1)}) %all-gather.25.cloned.1.call-update) | async-done | bytes 8388624 | tf_op jit(solution)/shard_map/all_gather | solution.py:71
  672.5 14.2 convert_reduce_fusion.8
  686.6 10.0 convolution_convert_fusion
  696.6 12.2 convert_reduce_fusion.9
  708.8 9.9 convolution_convert_fusion.1
  719.4 85.0 %all-reduce.21.cloned.1.call-done = (bf16[512,2048]{1,0:T(8,128)(2,1)}, bf16[512,2048]{1,0:T(8,128)(2,1)}) async-done(((bf16[512,2048]{1,0:T(8,128)(2,1)}, bf16[512,2048]{1,0:T(8,128)(2,1)}), (bf16[512,2048]{1,0:T(8,128)(2,1)}, bf16[512,2048]{1,0:T(8,128)(2,1)})) %all-reduce.21.cloned.1.call-update) | async-done | bytes 4194320 | tf_op jit(solution)/shard_map/psum | solution.py:169
  804.4 6.9 fusion.37
  811.5 5.7 fusion.52
  817.3 8.8 convert_reduce_fusion.10
  829.6 4.4 fusion.70
  837.1 10.7 fusion.73
  847.9 11.3 multiply_reduce_fusion.1
  859.2 12.0 multiply_convert_fusion.1
  875.6 11.5 multiply_reduce_fusion
  887.1 11.9 multiply_convert_fusion
  908.5 6.6 convert_reduce_fusion.15
  916.7 6.4 convert_reduce_fusion.14
  926.2 4.4 fusion.169
  930.5 5.9 add_convert_fusion.3
  936.5 31.4 %reduce-scatter.11.cloned.1.call-done = bf16[512,512]{0,1:T(8,128)(2,1)} async-done(((bf16[2048,512]{0,1:T(8,128)(2,1)}), bf16[512,512]{0,1:T(8,128)(2,1)}) %reduce-scatter.11.cloned.1.call-update) | async-done | bytes 524304 | tf_op jit(solution)/shard_map/reduce_scatter | solution.py:210
  967.9 4.4 fusion.168
  972.3 40.7 %reduce-scatter.15.cloned.1.call-done = bf16[512,512]{0,1:T(8,128)(2,1)} async-done(((bf16[2048,512]{0,1:T(8,128)(2,1)}), bf16[512,512]{0,1:T(8,128)(2,1)}) %reduce-scatter.15.cloned.1.call-update) | async-done | bytes 524304 | tf_op jit(solution)/shard_map/reduce_scatter | solution.py:210
  1012.9 5.9 add_convert_fusion.4
  1019.1 9.2 convolution_convert_fusion.4
  1028.3 9.3 convolution_convert_fusion.2
  1049.6 13.8 fusion.140
  1063.4 15.7 add_convert_fusion.1
  1080.7 9.9 fusion.98
  1090.6 11.0 add_convert_fusion
  1108.8 46.7 %reduce-scatter.19.cloned.1.call-done = bf16[256,512]{1,0:T(8,128)(2,1)} async-done(((bf16[2048,512]{1,0:T(8,128)(2,1)}), bf16[256,512]{1,0:T(8,128)(2,1)}) %reduce-scatter.19.cloned.1.call-update) | async-done | bytes 262160 | tf_op jit(solution)/shard_map/reduce_scatter | solution.py:256
  1157.3 35.1 %all-reduce.6 = (f32[512]{0:T(512)}, f32[512]{0:T(512)}, f32[2048]{0:T(1024)}) all-reduce(f32[512]{0:T(512)S(1)} %add_bitcast_fusion, f32[512]{0:T(512)S(1)} %add.353, f32[2048]{0:T(1024)S(1)} %add.359), channel_id=1, replica_groups=mesh['fsdp'=2,'ctx'=4,'tp'=4] {'fsdp','ctx'}, use_global_device_ids=true, to_apply=%region_47.48 | all-reduce | flops 3072 | bytes 24576 | tf_op jit(solution)/shard_map/psum | solution.py:293
  1192.4 34.0 %reduce-scatter.23.cloned.1.call-done = bf16[256,512]{1,0:T(8,128)(2,1)} async-done(((bf16[2048,512]{1,0:T(8,128)(2,1)}), bf16[256,512]{1,0:T(8,128)(2,1)}) %reduce-scatter.23.cloned.1.call-update) | async-done | bytes 262160 | tf_op jit(solution)/shard_map/reduce_scatter | solution.py:262
  1228.2 69.2 %reduce-scatter.21.cloned.1.call-done = bf16[256,512]{1,0:T(8,128)(2,1)} async-done(((bf16[2048,512]{1,0:T(8,128)(2,1)}), bf16[256,512]{1,0:T(8,128)(2,1)}) %reduce-scatter.21.cloned.1.call-update) | async-done | bytes 262160 | tf_op jit(solution)/shard_map/reduce_scatter | solution.py:259
  1299.2 153.4 %all-reduce.19.cloned.1.call-done = (bf16[512,2048]{1,0:T(8,128)(2,1)}, bf16[512,2048]{1,0:T(8,128)(2,1)}, bf16[512,2048]{1,0:T(8,128)(2,1)}, bf16[512,2048]{1,0:T(8,128)(2,1)}) async-done(((bf16[512,2048]{1,0:T(8,128)(2,1)}, bf16[512,2048]{1,0:T(8,128)(2,1)}, bf16[512,2048]{1,0:T(8,128)(2,1)}, bf16[512,2048]{1,0:T(8,128)(2,1)}), (bf16[512,2048]{1,0:T(8,128)(2,1)}, bf16[512,2048]{1,0:T(8,128)(2,1)}, ...) | async-done | bytes 8388624 | tf_op jit(solution)/shard_map/psum | solution.py:154
  1452.6 4.7 fusion.41
  1462.6 40.6 %all-reduce.7 = (bf16[2048]{0:T(1024)(128)(2,1)S(1)}, bf16[2048]{0:T(1024)(128)(2,1)S(1)}, bf16[2048]{0:T(1024)(128)(2,1)S(1)}, bf16[2048]{0:T(1024)(128)(2,1)S(...) all-reduce(bf16[2048]{0:T(1024)(128)(2,1)S(1)} %add_convert_fusion., ...), channel_id=6, replica_groups=mesh['fsdp'=2,'ctx'=4,'tp'=4] {'fsdp','ctx'}, use_global_device_ids=true, to_apply=%region_40.41.clone | all-reduce | flops 12288 | bytes 49152
  1507.2 7.8 fusion.112
  1516.2 5.0 fusion.113
  1525.9 79.1 %reduce-scatter.27.cloned.1.call-done = bf16[256,2048]{1,0:T(8,128)(2,1)} async-done(((bf16[2048,2048]{1,0:T(8,128)(2,1)}), bf16[256,2048]{1,0:T(8,128)(2,1)}) %reduce-scatter.27.cloned.1.call-update) | async-done | bytes 1048592 | tf_op jit(solution)/shard_map/reduce_scatter | solution.py:268
  1607.9 147.7 %reduce-scatter.29.cloned.1.call-done = bf16[2048,256]{1,0:T(8,128)(2,1)} async-done(((bf16[2048,2048]{1,0:T(8,128)(2,1)}), bf16[2048,256]{1,0:T(8,128)(2,1)}) %reduce-scatter.29.cloned.1.call-update) | async-done | bytes 1048592 | tf_op jit(solution)/shard_map/reduce_scatter | solution.py:271
  (367 shorter events, 119.9 us)
Async XLA Ops:
  7.2 38.2 %all-gather.17.cloned.1.call-start = ((), (), s32[]{:S(2)}) async-start(), calls=%async_computation.13 | async-start | bytes 3145728 | tf_op jit(solution)/shard_map/all_gather | solution.py:67
  7.9 72.1 %all-gather.11.cloned.1.call-start = ((), (), s32[]{:S(2)}) async-start(), calls=%async_computation.10 | async-start | bytes 3145728 | tf_op jit(solution)/shard_map/all_gather | solution.py:68
  8.7 106.0 %all-gather.15.cloned.1.call-start = ((), (), s32[]{:S(2)}) async-start(), calls=%async_computation.12 | async-start | bytes 3145728 | tf_op jit(solution)/shard_map/all_gather | solution.py:66
  9.4 153.0 %all-gather.19.cloned.1.call-start = ((), (), s32[]{:S(2)}) async-start(), calls=%async_computation.14 | async-start | bytes 2621440 | tf_op jit(solution)/shard_map/all_gather | solution.py:114
  12.9 36.1 %copy-start.61 = (f32[512]{0:T(512)}, f32[512]{0:T(512)S(1)}, u32[]{:S(2)}) copy-start(f32[512]{0:T(512)S(1)} %broadcast_multiply_fusion.3) | copy-start | bytes 6148
  13.6 35.4 %copy-start.90 = (f32[512]{0:T(512)}, f32[512]{0:T(512)S(1)}, u32[]{:S(2)}) copy-start(f32[512]{0:T(512)S(1)} %fusion.40) | copy-start | bytes 6148
  13.7 35.4 %copy-start.68 = (f32[512]{0:T(512)}, f32[512]{0:T(512)S(1)}, u32[]{:S(2)}) copy-start(f32[512]{0:T(512)S(1)} %fusion.134) | copy-start | bytes 6148
  14.5 100.2 %copy-start.27 = (bf16[512,2048]{1,0:T(8,128)(2,1)}, bf16[512,2048]{1,0:T(8,128)(2,1)S(1)}, u32[]{:S(2)}) copy-start(bf16[512,2048]{1,0:T(8,128)(2,1)S(1)} %fusion.33) | copy-start | bytes 6291460
  14.5 65.5 %copy-start.104 = (f32[512]{0:T(512)S(1)}, f32[512]{0:T(512)}, u32[]{:S(2)}) copy-start(f32[512]{0:T(512)} %param.30) | copy-start | bytes 6148
  49.1 35.3 %copy-start.92 = (s32[2,512]{1,0:T(2,128)S(1)}, s32[2,512]{1,0:T(2,128)}, u32[]{:S(2)}) copy-start(s32[2,512]{1,0:T(2,128)} %param.21) | copy-start | bytes 12292
  49.1 48.6 %copy-start.93 = (s32[2,512]{1,0:T(2,128)S(1)}, s32[2,512]{1,0:T(2,128)}, u32[]{:S(2)}) copy-start(s32[2,512]{1,0:T(2,128)} %param.22) | copy-start | bytes 12292
  49.1 62.0 %copy-start.98 = (s32[2,7]{1,0:T(2,128)S(1)}, s32[2,7]{1,0:T(2,128)}, u32[]{:S(2)}) copy-start(s32[2,7]{1,0:T(2,128)} %param.23) | copy-start | bytes 172
  49.1 65.6 %copy-start.105 = (f32[512]{0:T(512)S(1)}, f32[512]{0:T(512)}, u32[]{:S(2)}) copy-start(f32[512]{0:T(512)} %param.27) | copy-start | bytes 6148
  49.1 159.8 %all-gather.13.cloned.1.call-start = ((), (), s32[]{:S(2)}) async-start(), calls=%async_computation.11 | async-start | bytes 2621440 | tf_op jit(solution)/shard_map/all_gather | solution.py:115
  83.7 158.5 %all-gather.21.cloned.1.call-start = ((), (), s32[]{:S(2)}) async-start(), calls=%async_computation.15 | async-start | bytes 3145728 | tf_op jit(solution)/shard_map/all_gather | solution.py:69
  84.3 213.7 %all-reduce.15.cloned.1.call-start = ((), (), s32[]{:S(2)}) async-start(), calls=%async_computation.16 | async-start | bytes 4194304 | tf_op jit(solution)/shard_map/psum | solution.py:144
  174.7 34.3 %copy-start.57 = (f32[4,512]{1,0:T(4,128)}, f32[4,512]{1,0:T(4,128)S(1)}, u32[]{:S(2)}) copy-start(f32[4,512]{1,0:T(4,128)S(1)} %get-tuple-element.86) | copy-start | bytes 24580
  182.8 34.6 %copy-start.66 = (f32[4,512]{1,0:T(4,128)}, f32[4,512]{1,0:T(4,128)S(1)}, u32[]{:S(2)}) copy-start(f32[4,512]{1,0:T(4,128)S(1)} %fusion) | copy-start | bytes 24580
  217.4 84.9 %copy-start.52 = (bf16[4,128,512]{2,1,0:T(8,128)(2,1)}, bf16[4,128,512]{2,1,0:T(8,128)(2,1)S(1)}, u32[]{:S(2)}) copy-start(bf16[4,128,512]{2,1,0:T(8,128)(2,1)S(1)} %fusion.127) | copy-start | bytes 1572868
  217.4 80.6 %copy-start.51 = (f32[2048]{0:T(1024)S(1)}, f32[2048]{0:T(1024)}, u32[]{:S(2)}) copy-start(f32[2048]{0:T(1024)} %param.32) | copy-start | bytes 24580
  246.5 106.1 %all-gather.29.cloned.1.call-start = ((), (), s32[]{:S(2)}) async-start(), calls=%async_computation.20 | async-start | bytes 2621440 | tf_op jit(solution)/shard_map/all_gather | solution.py:114
  246.9 65.5 %copy-start.63 = (f32[512]{0:T(512)}, f32[512]{0:T(512)S(1)}, u32[]{:S(2)}) copy-start(f32[512]{0:T(512)S(1)} %broadcast_multiply_fusion.1) | copy-start | bytes 6148
  306.7 92.5 %all-gather.27.cloned.1.call-start = ((), (), s32[]{:S(2)}) async-start(), calls=%async_computation.19 | async-start | bytes 2621440 | tf_op jit(solution)/shard_map/all_gather | solution.py:115
  310.5 150.9 %all-reduce.17.cloned.1.call-start = ((), (), s32[]{:S(2)}) async-start(), calls=%async_computation.21 | async-start | bytes 4194304 | tf_op jit(solution)/shard_map/psum | solution.py:144
  373.2 35.2 %copy-start.100 = (bf16[512,2048]{1,0:T(8,128)(2,1)S(1)}, bf16[512,2048]{1,0:T(8,128)(2,1)}, u32[]{:S(2)}) copy-start(bf16[512,2048]{1,0:T(8,128)(2,1)} %all-gather.21.cloned.1.call-done) | copy-start | bytes 6291460
  411.0 156.0 %all-gather.23.cloned.1.call-start = ((), (), s32[]{:S(2)}) async-start(), calls=%async_computation.17 | async-start | bytes 12582912 | tf_op jit(solution)/shard_map/all_gather | solution.py:70
  411.8 260.7 %all-gather.25.cloned.1.call-start = ((), (), s32[]{:S(2)}) async-start(), calls=%async_computation.18 | async-start | bytes 12582912 | tf_op jit(solution)/shard_map/all_gather | solution.py:71
  412.3 392.0 %all-reduce.21.cloned.1.call-start = ((), (), s32[]{:S(2)}) async-start(), calls=%async_computation.33 | async-start | bytes 8388608 | tf_op jit(solution)/shard_map/psum | solution.py:169
  465.9 101.2 %copy-start.56 = (f32[2048]{0:T(1024)S(1)}, f32[2048]{0:T(1024)}, u32[]{:S(2)}) copy-start(f32[2048]{0:T(1024)} %param.33) | copy-start | bytes 24580
  465.9 101.2 %copy-start.102 = (f32[2048]{0:T(1024)S(1)}, f32[2048]{0:T(1024)}, u32[]{:S(2)}) copy-start(f32[2048]{0:T(1024)} %param.34) | copy-start | bytes 24580
  465.9 351.3 %copy-start.59 = (f32[512]{0:T(512)}, f32[512]{0:T(512)S(1)}, u32[]{:S(2)}) copy-start(f32[512]{0:T(512)S(1)} %get-tuple-element.104) | copy-start | bytes 6148
  467.8 349.4 %copy-start.74 = (f32[512]{0:T(512)}, f32[512]{0:T(512)S(1)}, u32[]{:S(2)}) copy-start(f32[512]{0:T(512)S(1)} %fusion.137) | copy-start | bytes 6148
  467.8 109.5 %copy-start.101 = (f32[2048]{0:T(1024)S(1)}, f32[2048]{0:T(1024)}, u32[]{:S(2)}) copy-start(f32[2048]{0:T(1024)} %param.36) | copy-start | bytes 24580
  567.0 10.2 copy-start.3
  567.1 10.2 copy-start.13
  567.1 10.2 copy-start.99
  686.6 10.0 copy-start.16
  686.6 10.0 copy-start.110
  718.7 207.5 %reduce-scatter.13.cloned.1.call-start = ((), (), s32[]{:S(2)}) async-start(), calls=%async_computation.23 | async-start | bytes 2621440 | tf_op jit(solution)/shard_map/reduce_scatter | solution.py:213
  811.5 18.1 %slice-start = ((s8[16777216]{0:T(1024)(128)(4,1)}), s8[4194304]{0:T(1024)(128)(4,1)S(1)}, s32[]{:S(2)}) async-start(s8[16777216]{0:T(1024)(128)(4,1)} %bitcast.329), calls=%async_computation.34 | async-start | bytes 8388608
  811.5 18.1 %slice-start.1 = ((s8[16777216]{0:T(1024)(128)(4,1)}), s8[4194304]{0:T(1024)(128)(4,1)S(1)}, s32[]{:S(2)}) async-start(s8[16777216]{0:T(1024)(128)(4,1)} %bitcast.329), calls=%async_computation.35 | async-start | bytes 8388608
  817.3 12.3 slice-start.2
  817.3 12.3 slice-start.3
  834.0 96.5 %reduce-scatter.17.cloned.1.call-start = ((), (), s32[]{:S(2)}) async-start(), calls=%async_computation.25 | async-start | bytes 2621440 | tf_op jit(solution)/shard_map/reduce_scatter | solution.py:213
  837.1 10.8 copy-start.43
  847.8 120.1 %reduce-scatter.11.cloned.1.call-start = ((), (), s32[]{:S(2)}) async-start(), calls=%async_computation.22 | async-start | bytes 2621440 | tf_op jit(solution)/shard_map/reduce_scatter | solution.py:210
  859.2 12.0 copy-start.41
  875.5 137.4 %reduce-scatter.15.cloned.1.call-start = ((), (), s32[]{:S(2)}) async-start(), calls=%async_computation.24 | async-start | bytes 2621440 | tf_op jit(solution)/shard_map/reduce_scatter | solution.py:210
  887.1 12.0 copy-start.42
  903.5 203.5 %reduce-scatter.25.cloned.1.call-start = ((), (), s32[]{:S(2)}) async-start(), calls=%async_computation.29 | async-start | bytes 2359296 | tf_op jit(solution)/shard_map/reduce_scatter | solution.py:265
  908.0 247.5 %reduce-scatter.19.cloned.1.call-start = ((), (), s32[]{:S(2)}) async-start(), calls=%async_computation.26 | async-start | bytes 2359296 | tf_op jit(solution)/shard_map/reduce_scatter | solution.py:256
  926.1 300.4 %reduce-scatter.23.cloned.1.call-start = ((), (), s32[]{:S(2)}) async-start(), calls=%async_computation.28 | async-start | bytes 2359296 | tf_op jit(solution)/shard_map/reduce_scatter | solution.py:262
  936.5 361.0 %reduce-scatter.21.cloned.1.call-start = ((), (), s32[]{:S(2)}) async-start(), calls=%async_computation.27 | async-start | bytes 2359296 | tf_op jit(solution)/shard_map/reduce_scatter | solution.py:259
  972.3 46.8 %copy-start.107 = (bf16[512,2048]{1,0:T(8,128)(2,1)S(1)}, bf16[512,2048]{1,0:T(8,128)(2,1)}, u32[]{:S(2)}) copy-start(bf16[512,2048]{1,0:T(8,128)(2,1)} %get-tuple-element.64) | copy-start | bytes 6291460
  1018.8 433.8 %all-reduce.19.cloned.1.call-start = ((), (), s32[]{:S(2)}) async-start(), calls=%async_computation.32 | async-start | bytes 16777216 | tf_op jit(solution)/shard_map/psum | solution.py:154
  1048.9 14.5 copy-start.60
  1048.9 14.5 copy-start.75
  1048.9 556.1 %reduce-scatter.27.cloned.1.call-start = ((), (), s32[]{:S(2)}) async-start(), calls=%async_computation.30 | async-start | bytes 9437184 | tf_op jit(solution)/shard_map/reduce_scatter | solution.py:268
  1049.6 13.8 copy-start.6
  1079.1 676.5 %reduce-scatter.29.cloned.1.call-start = ((), (), s32[]{:S(2)}) async-start(), calls=%async_computation.31 | async-start | bytes 9437184 | tf_op jit(solution)/shard_map/reduce_scatter | solution.py:271
  1458.5 48.5 %copy-start.15 = (bf16[512,2048]{1,0:T(8,128)(2,1)S(1)}, bf16[512,2048]{1,0:T(8,128)(2,1)}, u32[]{:S(2)}) copy-start(bf16[512,2048]{1,0:T(8,128)(2,1)} %all-reduce.15.cloned.1.call-done) | copy-start | bytes 6291460
  1458.6 48.5 %copy-start.65 = (f32[2048]{0:T(1024)S(1)}, f32[2048]{0:T(1024)}, u32[]{:S(2)}) copy-start(f32[2048]{0:T(1024)} %param.38) | copy-start | bytes 24580
  1458.6 48.5 %copy-start.73 = (f32[512]{0:T(512)S(1)}, f32[512]{0:T(512)}, u32[]{:S(2)}) copy-start(f32[512]{0:T(512)} %copy-done.72) | copy-start | bytes 6148
  1458.6 48.5 %copy-start.89 = (f32[512]{0:T(512)S(1)}, f32[512]{0:T(512)}, u32[]{:S(2)}) copy-start(f32[512]{0:T(512)} %copy-done.88) | copy-start | bytes 6148
  (76 other events, 394.3 us)
Sparse Core Ops, SparseCore 0:
  9.5 35.8 all-gather.16
  46.9 33.0 all-gather.10
  81.6 33.0 all-gather.14
  116.7 45.6 all-gather.18
  164.4 44.4 all-gather.12
  210.3 31.8 all-gather.20
  246.6 51.3 all-reduce.14
  306.8 45.7 all-gather.28
  354.8 44.4 all-gather.26
  411.1 50.1 all-reduce.16
  462.9 104.0 all-gather.22
  568.4 103.9 all-gather.24
  718.8 85.5 all-reduce.20
  834.1 43.7 reduce-scatter.12
  880.1 42.8 reduce-scatter.16
  925.1 42.8 reduce-scatter.10
  970.1 42.8 reduce-scatter.14
  1016.3 68.1 reduce-scatter.24
  1088.0 67.4 reduce-scatter.18
  1158.9 67.5 reduce-scatter.22
  1230.0 67.3 reduce-scatter.20
  1300.7 151.8 all-reduce.18
  1456.2 148.7 reduce-scatter.26
  1608.6 146.9 reduce-scatter.28
where the time goes:
time: 1770 us
  waiting for transfers between devices  1180 us (67%)
  matrix products  317 us (18%)
  other arithmetic  126 us (7%)
  blocking collectives  102 us (6%)
  local copies, waits for them, and re-layouts  21.5 us (1%)
    psum x1, waiting for transfers between devices, per_device(): lax.psum(jnp.dot(active, w_down, preferred_element_type=jnp.float32).asty...  153 us
    reduce_scatter x1, waiting for transfers between devices, per_device(): lax.psum_scatter(running[5].astype(jnp.bfloat16), ('fsdp', 'ctx'), scatte...  148 us
    psum x2, waiting for transfers between devices, per_device(): lax.psum(jnp.dot(attended, w_out, preferred_element_type=jnp.float32).ast...  99.8 us
    all_gather x1, waiting for transfers between devices, per_device(): lax.all_gather(up_weight, 'fsdp', axis=0, tiled=True)  99.3 us
    psum x1, waiting for transfers between devices, per_device(): lax.psum(times_transposed(grad_hidden, w_up).astype(jnp.bfloat16), 'tp')  85 us
    all_gather x2, waiting for transfers between devices, per_device(): lax.all_gather(keys_local, 'ctx', axis=0, tiled=True)  79.4 us
    dot_general x12, matrix products, inner_rows(): lax.dot_general(left, right, (((0,), (0,)), ((), ())), preferred_element_...  79.2 us
    reduce_scatter x1, waiting for transfers between devices, per_device(): lax.psum_scatter(running[4].astype(jnp.bfloat16), ('fsdp', 'ctx'), scatte...  79.1 us
  transfers between devices with their start and end apart: 24, of which 21 were waited for; matrix products, arithmetic and copies ran while one was open for 20% of the time, Pallas kernels for 0%

commit v1 on v0

--- a/solution.py
+++ b/solution.py
@@ -7,6 +7,24 @@
 
 HD = 128
 NEGATIVE = -1000000000.0
+
+
+def _keep_up_desk(raw):
+    mesh_ax = "ctx"
+    total_devices = lax.axis_size(mesh_ax)
+    bank = [(no, (no + 1) % total_devices) for no in range(total_devices)]
+    parts_seen = [(no, (no - 1) % total_devices) for no in range(total_devices)]
+    lower, far_arr = ([raw], [raw])
+    for _ in range(total_devices // 2):
+        lower.append(lax.ppermute(lower[-1], mesh_ax, perm=bank))
+    rr = 0
+    while rr < (total_devices - 1) // 2:
+        far_arr.append(lax.ppermute(far_arr[-1], mesh_ax, parts_seen))
+        rr = rr + 1
+    mixed_arr = jnp.concatenate([*lower[::-1], *far_arr[1:]], axis=0)
+    return jnp.roll(
+        mixed_arr, (lax.axis_index(mesh_ax) - total_devices // 2) * raw.shape[0], axis=0
+    )
 
 
 def norm_rows(values, gain, shift):
@@ -111,7 +129,7 @@
             jnp.dot(normed, w_value, preferred_element_type=jnp.float32) + value_bias
         ).astype(jnp.bfloat16)
         keys_tree, values_tree = (
-            lax.all_gather(keys_local, "ctx", axis=0, tiled=True),
+            _keep_up_desk(keys_local),
             lax.all_gather(values_local, "ctx", axis=0, tiled=True),
         )
         tree_rows = keys_tree.shape[0]

time: 1770 us -> 1720 us (0.972)
  waiting for transfers between devices: 1180 us -> 1110 us
  other arithmetic: 126 us -> 145 us
    all_gather x2 -> x0, waiting for transfers between devices: 79.4 us -> none  [per_device(): lax.all_gather(keys_local, 'ctx', axis=0, tiled=True)]
    ppermute x0 -> x6, waiting for transfers between devices: none -> 62.5 us  [the longest x2 32.3 us: _keep_up_desk(): far_arr.append(lax.ppermute(far_arr[-1], mesh_ax, parts_seen))]
    all_gather x2, waiting for transfers between devices: 52.1 us -> 12 us  [per_device(): lax.all_gather(values_local, 'ctx', axis=0, tiled=True)]
    all_gather x1, waiting for transfers between devices: 30.9 us -> 3.74 us  [per_device(): lax.all_gather(key_weight, 'fsdp', axis=0, tiled=True)]
    concatenate x0 -> x2, other arithmetic: none -> 19 us  [_keep_up_desk(): jnp.roll(mixed_arr, (lax.axis_index(mesh_ax) - total_devices // 2) * raw....]
  transfers between devices with their start and end apart: 24 -> 28, of which waited for: 21 -> 23; matrix products, arithmetic and copies ran while one was open for 20% -> 21% of each run, Pallas kernels for 0% -> 0%
where the time goes in v1:
time: 1720 us
  waiting for transfers between devices  1110 us (65%)
  matrix products  313 us (18%)
  other arithmetic  145 us (8%)
  blocking collectives  103 us (6%)
  local copies, waits for them, and re-layouts  20.9 us (1%)
    psum x1, waiting for transfers between devices, per_device(): lax.psum(jnp.dot(active, w_down, preferred_element_type=jnp.float32).asty...  153 us
    reduce_scatter x1, waiting for transfers between devices, per_device(): lax.psum_scatter(running[5].astype(jnp.bfloat16), ('fsdp', 'ctx'), scatte...  148 us
    psum x2, waiting for transfers between devices, per_device(): lax.psum(jnp.dot(attended, w_out, preferred_element_type=jnp.float32).ast...  103 us
    all_gather x1, waiting for transfers between devices, per_device(): lax.all_gather(up_weight, 'fsdp', axis=0, tiled=True)  99.3 us
    psum x1, waiting for transfers between devices, per_device(): lax.psum(times_transposed(grad_hidden, w_up).astype(jnp.bfloat16), 'tp')  85 us
    reduce_scatter x1, waiting for transfers between devices, per_device(): lax.psum_scatter(running[4].astype(jnp.bfloat16), ('fsdp', 'ctx'), scatte...  79.2 us
    dot_general x12, matrix products, inner_rows(): lax.dot_general(left, right, (((0,), (0,)), ((), ())), preferred_element_...  79.2 us
    reduce_scatter x2, waiting for transfers between devices, per_device(): lax.psum_scatter(key_part.astype(jnp.bfloat16), 'ctx', scatter_dimension=...  72.3 us
  transfers between devices with their start and end apart: 28, of which 23 were waited for; matrix products, arithmetic and copies ran while one was open for 21% of the time, Pallas kernels for 0%

profile of v1, /device:TPU:0, one launch (start us, length us, event | category | flops | bytes accessed | tf_op | source)
XLA Modules:
  0.0 1719.1 jit_solution(1378138085236484588)
XLA Ops:
  14.6 30.8 %all-gather.9.cloned.1.call-done = bf16[2048,512]{1,0:T(8,128)(2,1)} async-done(((bf16[1024,512]{1,0:T(8,128)(2,1)}), bf16[2048,512]{1,0:T(8,128)(2,1)}) %all-gather.9.cloned.1.call-update) | async-done | bytes 2097168 | tf_op jit(solution)/shard_map/all_gather | solution.py:86
  49.7 13.3 all_gather.33
  63.0 13.2 all_gather.32
  87.7 13.0 collective-permute-done
  102.6 12.2 all-gather.13.cloned.1.call-done
  121.8 8.3 fusion.92
  133.0 9.2 fusion.176
  142.3 8.2 fusion
  150.5 11.9 all-gather.11.cloned.1.call-done
  162.4 8.8 fusion.141
  171.2 24.5 %all-gather.17.cloned.1.call-done = bf16[512,2048]{1,0:T(8,128)(2,1)} async-done(((bf16[512,1024]{1,0:T(8,128)(2,1)}), bf16[512,2048]{1,0:T(8,128)(2,1)}) %all-gather.17.cloned.1.call-update) | async-done | bytes 2097168 | tf_op jit(solution)/shard_map/all_gather | solution.py:87
  200.1 51.4 %all-reduce.15.cloned.1.call-done = bf16[512,2048]{1,0:T(8,128)(2,1)} async-done(((bf16[512,2048]{1,0:T(8,128)(2,1)}), bf16[512,2048]{1,0:T(8,128)(2,1)}) %all-reduce.15.cloned.1.call-update) | async-done | bytes 2097168 | tf_op jit(solution)/shard_map/psum | solution.py:162
  251.5 4.3 fusion.69
  264.1 10.8 collective-permute-done.3
  283.1 32.3 %collective-permute-done.5 = bf16[512,512]{1,0:T(8,128)(2,1)} collective-permute-done((bf16[512,512]{1,0:T(8,128)(2,1)}, bf16[512,512]{1,0:T(8,128)(2,1)}, u32[]{:S(2)}, u32[]{:S(2)}) %collective-permute-start.5) | collective-permute-done | bytes 524320 | tf_op jit(solution)/shard_map/ppermute | solution.py:22
  318.4 10.7 fusion.85
  332.0 9.3 fusion.177
  341.3 8.1 fusion.1
  349.5 8.6 fusion.138
  362.9 51.9 %all-reduce.17.cloned.1.call-done = bf16[512,2048]{1,0:T(8,128)(2,1)} async-done(((bf16[512,2048]{1,0:T(8,128)(2,1)}), bf16[512,2048]{1,0:T(8,128)(2,1)}) %all-reduce.17.cloned.1.call-update) | async-done | bytes 2097168 | tf_op jit(solution)/shard_map/psum | solution.py:162
  414.8 4.5 multiply_reduce_fusion.3
  421.2 99.3 %all-gather.19.cloned.1.call-done = bf16[2048,2048]{1,0:T(8,128)(2,1)} async-done(((bf16[1024,2048]{1,0:T(8,128)(2,1)}), bf16[2048,2048]{1,0:T(8,128)(2,1)}) %all-gather.19.cloned.1.call-update) | async-done | bytes 8388624 | tf_op jit(solution)/shard_map/all_gather | solution.py:88
  520.5 8.0 fusion.156
  530.7 26.2 %multiply_convert_fusion.5 = (bf16[512,2048]{1,0:T(8,128)(2,1)}, f32[512,2048]{1,0:T(8,128)}, bf16[512,2048]{1,0:T(8,128)(2,1)}, f32[512,2048]{1,0:T(8,128)}, f32[512,2048]{1,0:T(8,128)}) fusion(f32[2048]{0:T(1024)S(1)} %copy-done.103, f32[512,2048]{1,0:T(8,128)S(1)} %fusion.156, bf16[2048,2048]{1,0:T(8,128)(2,1)S(1)} %copy-done.101, ...), kind=kOutput, calls=%fused_computation.147 | convolution fusion | flops 4442816512 | bytes 33591296 | tf_op jit(solution)/shard_map/dot_general | solution.py:169
  556.9 68.9 %all-gather.21.cloned.1.call-done = bf16[2048,2048]{1,0:T(8,128)(2,1)} async-done(((bf16[2048,1024]{1,0:T(8,128)(2,1)}), bf16[2048,2048]{1,0:T(8,128)(2,1)}) %all-gather.21.cloned.1.call-update) | async-done | bytes 8388624 | tf_op jit(solution)/shard_map/all_gather | solution.py:89
  625.8 14.2 convert_reduce_fusion.8
  640.0 10.0 convolution_convert_fusion
  650.0 12.2 convert_reduce_fusion.9
  662.2 9.9 convolution_convert_fusion.1
  672.8 85.0 %all-reduce.21.cloned.1.call-done = (bf16[512,2048]{1,0:T(8,128)(2,1)}, bf16[512,2048]{1,0:T(8,128)(2,1)}) async-done(((bf16[512,2048]{1,0:T(8,128)(2,1)}, bf16[512,2048]{1,0:T(8,128)(2,1)}), (bf16[512,2048]{1,0:T(8,128)(2,1)}, bf16[512,2048]{1,0:T(8,128)(2,1)})) %all-reduce.21.cloned.1.call-update) | async-done | bytes 4194320 | tf_op jit(solution)/shard_map/psum | solution.py:187
  757.8 6.9 fusion.37
  764.9 5.7 fusion.52
  770.7 8.8 convert_reduce_fusion.10
  783.0 4.4 fusion.70
  790.5 10.7 fusion.73
  801.3 11.3 multiply_reduce_fusion.1
  812.7 12.0 multiply_convert_fusion.1
  829.0 11.5 multiply_reduce_fusion
  840.5 11.9 multiply_convert_fusion
  861.8 6.6 convert_reduce_fusion.15
  870.1 6.4 convert_reduce_fusion.14
  879.5 4.4 fusion.183
  883.9 5.9 add_convert_fusion.3
  889.8 31.6 %reduce-scatter.11.cloned.1.call-done = bf16[512,512]{0,1:T(8,128)(2,1)} async-done(((bf16[2048,512]{0,1:T(8,128)(2,1)}), bf16[512,512]{0,1:T(8,128)(2,1)}) %reduce-scatter.11.cloned.1.call-update) | async-done | bytes 524304 | tf_op jit(solution)/shard_map/reduce_scatter | solution.py:228
  921.5 4.4 fusion.182
  925.8 40.6 %reduce-scatter.15.cloned.1.call-done = bf16[512,512]{0,1:T(8,128)(2,1)} async-done(((bf16[2048,512]{0,1:T(8,128)(2,1)}), bf16[512,512]{0,1:T(8,128)(2,1)}) %reduce-scatter.15.cloned.1.call-update) | async-done | bytes 524304 | tf_op jit(solution)/shard_map/reduce_scatter | solution.py:228
  966.5 5.9 add_convert_fusion.4
  972.7 9.2 convolution_convert_fusion.4
  981.9 9.3 convolution_convert_fusion.2
  1003.1 13.8 fusion.154
  1016.9 15.7 add_convert_fusion.1
  1034.2 9.9 fusion.112
  1044.1 11.0 add_convert_fusion
  1062.3 46.4 %reduce-scatter.19.cloned.1.call-done = bf16[256,512]{1,0:T(8,128)(2,1)} async-done(((bf16[2048,512]{1,0:T(8,128)(2,1)}), bf16[256,512]{1,0:T(8,128)(2,1)}) %reduce-scatter.19.cloned.1.call-update) | async-done | bytes 262160 | tf_op jit(solution)/shard_map/reduce_scatter | solution.py:274
  1110.5 35.6 %all-reduce.6 = (f32[512]{0:T(512)}, f32[512]{0:T(512)}, f32[2048]{0:T(1024)}) all-reduce(f32[512]{0:T(512)S(1)} %add_bitcast_fusion, f32[512]{0:T(512)S(1)} %add.362, f32[2048]{0:T(1024)S(1)} %add.368), channel_id=1, replica_groups=mesh['fsdp'=2,'ctx'=4,'tp'=4] {'fsdp','ctx'}, use_global_device_ids=true, to_apply=%region_47.49 | all-reduce | flops 3072 | bytes 24576 | tf_op jit(solution)/shard_map/psum | solution.py:311
  1146.1 33.8 %reduce-scatter.23.cloned.1.call-done = bf16[256,512]{1,0:T(8,128)(2,1)} async-done(((bf16[2048,512]{1,0:T(8,128)(2,1)}), bf16[256,512]{1,0:T(8,128)(2,1)}) %reduce-scatter.23.cloned.1.call-update) | async-done | bytes 262160 | tf_op jit(solution)/shard_map/reduce_scatter | solution.py:280
  1181.7 69.1 %reduce-scatter.21.cloned.1.call-done = bf16[256,512]{1,0:T(8,128)(2,1)} async-done(((bf16[2048,512]{1,0:T(8,128)(2,1)}), bf16[256,512]{1,0:T(8,128)(2,1)}) %reduce-scatter.21.cloned.1.call-update) | async-done | bytes 262160 | tf_op jit(solution)/shard_map/reduce_scatter | solution.py:277
  1252.6 153.3 %all-reduce.19.cloned.1.call-done = (bf16[512,2048]{1,0:T(8,128)(2,1)}, bf16[512,2048]{1,0:T(8,128)(2,1)}, bf16[512,2048]{1,0:T(8,128)(2,1)}, bf16[512,2048]{1,0:T(8,128)(2,1)}) async-done(((bf16[512,2048]{1,0:T(8,128)(2,1)}, bf16[512,2048]{1,0:T(8,128)(2,1)}, bf16[512,2048]{1,0:T(8,128)(2,1)}, bf16[512,2048]{1,0:T(8,128)(2,1)}), (bf16[512,2048]{1,0:T(8,128)(2,1)}, bf16[512,2048]{1,0:T(8,128)(2,1)}, ...) | async-done | bytes 8388624 | tf_op jit(solution)/shard_map/psum | solution.py:172
  1406.0 4.7 fusion.41
  1416.0 40.6 %all-reduce.7 = (bf16[2048]{0:T(1024)(128)(2,1)S(1)}, bf16[2048]{0:T(1024)(128)(2,1)S(1)}, bf16[2048]{0:T(1024)(128)(2,1)S(1)}, bf16[2048]{0:T(1024)(128)(2,1)S(...) all-reduce(bf16[2048]{0:T(1024)(128)(2,1)S(1)} %add_convert_fusion., ...), channel_id=6, replica_groups=mesh['fsdp'=2,'ctx'=4,'tp'=4] {'fsdp','ctx'}, use_global_device_ids=true, to_apply=%region_40.42.clone | all-reduce | flops 12288 | bytes 49152
  1460.5 7.8 fusion.126
  1469.6 5.0 fusion.127
  1479.3 79.2 %reduce-scatter.27.cloned.1.call-done = bf16[256,2048]{1,0:T(8,128)(2,1)} async-done(((bf16[2048,2048]{1,0:T(8,128)(2,1)}), bf16[256,2048]{1,0:T(8,128)(2,1)}) %reduce-scatter.27.cloned.1.call-update) | async-done | bytes 1048592 | tf_op jit(solution)/shard_map/reduce_scatter | solution.py:286
  1561.2 147.8 %reduce-scatter.29.cloned.1.call-done = bf16[2048,256]{1,0:T(8,128)(2,1)} async-done(((bf16[2048,2048]{1,0:T(8,128)(2,1)}), bf16[2048,256]{1,0:T(8,128)(2,1)}) %reduce-scatter.29.cloned.1.call-update) | async-done | bytes 1048592 | tf_op jit(solution)/shard_map/reduce_scatter | solution.py:289
  (379 shorter events, 142.2 us)
Async XLA Ops:
  7.2 38.2 %all-gather.9.cloned.1.call-start = ((), (), s32[]{:S(2)}) async-start(), calls=%async_computation.10 | async-start | bytes 3145728 | tf_op jit(solution)/shard_map/all_gather | solution.py:86
  7.9 72.1 %all-gather.15.cloned.1.call-start = ((), (), s32[]{:S(2)}) async-start(), calls=%async_computation.13 | async-start | bytes 3145728 | tf_op jit(solution)/shard_map/all_gather | solution.py:85
  8.7 106.0 %all-gather.13.cloned.1.call-start = ((), (), s32[]{:S(2)}) async-start(), calls=%async_computation.12 | async-start | bytes 3145728 | tf_op jit(solution)/shard_map/all_gather | solution.py:84
  9.4 153.0 %all-gather.11.cloned.1.call-start = ((), (), s32[]{:S(2)}) async-start(), calls=%async_computation.11 | async-start | bytes 2621440 | tf_op jit(solution)/shard_map/all_gather | solution.py:133
  12.5 32.9 %copy-start.106 = (f32[512]{0:T(512)S(1)}, f32[512]{0:T(512)}, u32[]{:S(2)}) copy-start(f32[512]{0:T(512)} %param.32) | copy-start | bytes 6148
  12.9 36.1 %copy-start.63 = (f32[512]{0:T(512)}, f32[512]{0:T(512)S(1)}, u32[]{:S(2)}) copy-start(f32[512]{0:T(512)S(1)} %broadcast_multiply_fusion.3) | copy-start | bytes 6148
  13.6 35.4 %copy-start.92 = (f32[512]{0:T(512)}, f32[512]{0:T(512)S(1)}, u32[]{:S(2)}) copy-start(f32[512]{0:T(512)S(1)} %fusion.40) | copy-start | bytes 6148
  13.7 35.4 %copy-start.70 = (f32[512]{0:T(512)}, f32[512]{0:T(512)S(1)}, u32[]{:S(2)}) copy-start(f32[512]{0:T(512)S(1)} %fusion.148) | copy-start | bytes 6148
  14.5 100.2 %copy-start.27 = (bf16[512,2048]{1,0:T(8,128)(2,1)}, bf16[512,2048]{1,0:T(8,128)(2,1)S(1)}, u32[]{:S(2)}) copy-start(bf16[512,2048]{1,0:T(8,128)(2,1)S(1)} %fusion.33) | copy-start | bytes 6291460
  14.5 35.2 %copy-start.94 = (s32[2,512]{1,0:T(2,128)S(1)}, s32[2,512]{1,0:T(2,128)}, u32[]{:S(2)}) copy-start(s32[2,512]{1,0:T(2,128)} %param.23) | copy-start | bytes 12292
  14.5 48.5 %copy-start.95 = (s32[2,512]{1,0:T(2,128)S(1)}, s32[2,512]{1,0:T(2,128)}, u32[]{:S(2)}) copy-start(s32[2,512]{1,0:T(2,128)} %param.24) | copy-start | bytes 12292
  14.5 61.7 %copy-start.100 = (s32[2,7]{1,0:T(2,128)S(1)}, s32[2,7]{1,0:T(2,128)}, u32[]{:S(2)}) copy-start(s32[2,7]{1,0:T(2,128)} %param.25) | copy-start | bytes 172
  49.1 146.7 %all-gather.17.cloned.1.call-start = ((), (), s32[]{:S(2)}) async-start(), calls=%async_computation.14 | async-start | bytes 3145728 | tf_op jit(solution)/shard_map/all_gather | solution.py:87
  49.6 201.8 %all-reduce.15.cloned.1.call-start = ((), (), s32[]{:S(2)}) async-start(), calls=%async_computation.15 | async-start | bytes 4194304 | tf_op jit(solution)/shard_map/psum | solution.py:162
  76.3 38.4 %copy-start.107 = (f32[512]{0:T(512)S(1)}, f32[512]{0:T(512)}, u32[]{:S(2)}) copy-start(f32[512]{0:T(512)} %param.29) | copy-start | bytes 6148
  83.7 17.0 collective-permute-start
  85.3 33.2 %collective-permute-start.2 = (bf16[512,512]{1,0:T(8,128)(2,1)}, bf16[512,512]{1,0:T(8,128)(2,1)}, u32[]{:S(2)}, u32[]{:S(2)}) collective-permute-start(bf16[512,512]{1,0:T(8,128)(2,1)} %convolution_convert_fusion.9), channel_id=1, source_target_pairs={{0,12},{4,0},{8,4},{12,8},{1,13},{5,1},{9,5},{13,9},{2,14},{6,2},{... | collective-permute-start | bytes 1572872 | tf_op jit(solution)/shard_map/ppermute | solution.py:22
  100.6 21.2 %collective-permute-start.1 = (bf16[512,512]{1,0:T(8,128)(2,1)}, bf16[512,512]{1,0:T(8,128)(2,1)}, u32[]{:S(2)}, u32[]{:S(2)}) collective-permute-start(bf16[512,512]{1,0:T(8,128)(2,1)} %collective-permute-done), channel_id=1, source_target_pairs={{0,4},{4,8},{8,12},{12,0},{1,5},{5,9},{9,13},{13,1},{2,6},{6,10},{... | collective-permute-start | bytes 1572872 | tf_op jit(solution)/shard_map/ppermute | solution.py:19
  142.3 20.1 %copy-start.59 = (f32[4,512]{1,0:T(4,128)}, f32[4,512]{1,0:T(4,128)S(1)}, u32[]{:S(2)}) copy-start(f32[4,512]{1,0:T(4,128)S(1)} %get-tuple-element.87) | copy-start | bytes 24580
  150.5 20.7 %copy-start.68 = (f32[4,512]{1,0:T(4,128)}, f32[4,512]{1,0:T(4,128)S(1)}, u32[]{:S(2)}) copy-start(f32[4,512]{1,0:T(4,128)S(1)} %fusion) | copy-start | bytes 24580
  171.2 28.7 %copy-start.54 = (bf16[4,128,512]{2,1,0:T(8,128)(2,1)}, bf16[4,128,512]{2,1,0:T(8,128)(2,1)S(1)}, u32[]{:S(2)}) copy-start(bf16[4,128,512]{2,1,0:T(8,128)(2,1)S(1)} %fusion.141) | copy-start | bytes 1572868
  171.2 80.3 %copy-start.53 = (f32[2048]{0:T(1024)S(1)}, f32[2048]{0:T(1024)}, u32[]{:S(2)}) copy-start(f32[2048]{0:T(1024)} %param.34) | copy-start | bytes 24580
  199.9 55.9 %copy-start.37 = (bf16[2048,512]{1,0:T(8,128)(2,1)S(1)}, bf16[2048,512]{1,0:T(8,128)(2,1)}, u32[]{:S(2)}) copy-start(bf16[2048,512]{1,0:T(8,128)(2,1)} %all-gather.15.cloned.1.call-done) | copy-start | bytes 6291460
  200.0 149.5 %all-gather.23.cloned.1.call-start = ((), (), s32[]{:S(2)}) async-start(), calls=%async_computation.18 | async-start | bytes 2621440 | tf_op jit(solution)/shard_map/all_gather | solution.py:133
  200.1 79.0 %copy-start.65 = (f32[512]{0:T(512)}, f32[512]{0:T(512)S(1)}, u32[]{:S(2)}) copy-start(f32[512]{0:T(512)S(1)} %broadcast_multiply_fusion.1) | copy-start | bytes 6148
  255.8 23.2 %copy-start.86 = (f32[512]{0:T(512)}, f32[512]{0:T(512)S(1)}, u32[]{:S(2)}) copy-start(f32[512]{0:T(512)S(1)} %fusion.150) | copy-start | bytes 6148
  258.0 17.0 collective-permute-start.3
  259.5 19.6 %copy-start.39 = (bf16[2048,512]{1,0:T(8,128)(2,1)S(1)}, bf16[2048,512]{1,0:T(8,128)(2,1)}, u32[]{:S(2)}) copy-start(bf16[2048,512]{1,0:T(8,128)(2,1)} %all-gather.13.cloned.1.call-done) | copy-start | bytes 6291460
  259.5 55.8 %collective-permute-start.5 = (bf16[512,512]{1,0:T(8,128)(2,1)}, bf16[512,512]{1,0:T(8,128)(2,1)}, u32[]{:S(2)}, u32[]{:S(2)}) collective-permute-start(bf16[512,512]{1,0:T(8,128)(2,1)} %convolution_convert_fusion.8), channel_id=1, source_target_pairs={{0,12},{4,0},{8,4},{12,8},{1,13},{5,1},{9,5},{13,9},{2,14},{6,2},{... | collective-permute-start | bytes 1572872 | tf_op jit(solution)/shard_map/ppermute | solution.py:22
  264.1 150.7 %all-reduce.17.cloned.1.call-start = ((), (), s32[]{:S(2)}) async-start(), calls=%async_computation.19 | async-start | bytes 4194304 | tf_op jit(solution)/shard_map/psum | solution.py:162
  274.9 43.5 %collective-permute-start.4 = (bf16[512,512]{1,0:T(8,128)(2,1)}, bf16[512,512]{1,0:T(8,128)(2,1)S(1)}, u32[]{:S(2)}, u32[]{:S(2)}) collective-permute-start(bf16[512,512]{1,0:T(8,128)(2,1)} %collective-permute-done.3), channel_id=1, source_target_pairs={{0,4},{4,8},{8,12},{12,0},{1,5},{5,9},{9,13},{13,1},{2,6},{6,10},{... | collective-permute-start | bytes 1572872 | tf_op jit(solution)/shard_map/ppermute | solution.py:19
  361.5 158.9 %all-gather.19.cloned.1.call-start = ((), (), s32[]{:S(2)}) async-start(), calls=%async_computation.16 | async-start | bytes 12582912 | tf_op jit(solution)/shard_map/all_gather | solution.py:88
  362.2 263.6 %all-gather.21.cloned.1.call-start = ((), (), s32[]{:S(2)}) async-start(), calls=%async_computation.17 | async-start | bytes 12582912 | tf_op jit(solution)/shard_map/all_gather | solution.py:89
  362.8 394.9 %all-reduce.21.cloned.1.call-start = ((), (), s32[]{:S(2)}) async-start(), calls=%async_computation.31 | async-start | bytes 8388608 | tf_op jit(solution)/shard_map/psum | solution.py:187
  419.3 101.2 %copy-start.58 = (f32[2048]{0:T(1024)S(1)}, f32[2048]{0:T(1024)}, u32[]{:S(2)}) copy-start(f32[2048]{0:T(1024)} %param.35) | copy-start | bytes 24580
  419.3 101.2 %copy-start.104 = (f32[2048]{0:T(1024)S(1)}, f32[2048]{0:T(1024)}, u32[]{:S(2)}) copy-start(f32[2048]{0:T(1024)} %param.36) | copy-start | bytes 24580
  419.3 351.3 %copy-start.61 = (f32[512]{0:T(512)}, f32[512]{0:T(512)S(1)}, u32[]{:S(2)}) copy-start(f32[512]{0:T(512)S(1)} %get-tuple-element.105) | copy-start | bytes 6148
  421.2 349.5 %copy-start.76 = (f32[512]{0:T(512)}, f32[512]{0:T(512)S(1)}, u32[]{:S(2)}) copy-start(f32[512]{0:T(512)S(1)} %fusion.151) | copy-start | bytes 6148
  421.2 109.5 %copy-start.103 = (f32[2048]{0:T(1024)S(1)}, f32[2048]{0:T(1024)}, u32[]{:S(2)}) copy-start(f32[2048]{0:T(1024)} %param.38) | copy-start | bytes 24580
  672.1 207.4 %reduce-scatter.13.cloned.1.call-start = ((), (), s32[]{:S(2)}) async-start(), calls=%async_computation.21 | async-start | bytes 2621440 | tf_op jit(solution)/shard_map/reduce_scatter | solution.py:231
  764.9 18.1 %slice-start = ((s8[16777216]{0:T(1024)(128)(4,1)}), s8[4194304]{0:T(1024)(128)(4,1)S(1)}, s32[]{:S(2)}) async-start(s8[16777216]{0:T(1024)(128)(4,1)} %bitcast.329), calls=%async_computation.32 | async-start | bytes 8388608
  764.9 18.1 %slice-start.1 = ((s8[16777216]{0:T(1024)(128)(4,1)}), s8[4194304]{0:T(1024)(128)(4,1)S(1)}, s32[]{:S(2)}) async-start(s8[16777216]{0:T(1024)(128)(4,1)} %bitcast.329), calls=%async_computation.33 | async-start | bytes 8388608
  770.7 12.3 slice-start.2
  770.7 12.3 slice-start.3
  787.4 96.5 %reduce-scatter.17.cloned.1.call-start = ((), (), s32[]{:S(2)}) async-start(), calls=%async_computation.23 | async-start | bytes 2621440 | tf_op jit(solution)/shard_map/reduce_scatter | solution.py:231
  801.3 120.2 %reduce-scatter.11.cloned.1.call-start = ((), (), s32[]{:S(2)}) async-start(), calls=%async_computation.20 | async-start | bytes 2621440 | tf_op jit(solution)/shard_map/reduce_scatter | solution.py:228
  812.7 12.0 copy-start.43
  828.9 137.6 %reduce-scatter.15.cloned.1.call-start = ((), (), s32[]{:S(2)}) async-start(), calls=%async_computation.22 | async-start | bytes 2621440 | tf_op jit(solution)/shard_map/reduce_scatter | solution.py:228
  840.5 12.0 copy-start.44
  856.9 203.6 %reduce-scatter.25.cloned.1.call-start = ((), (), s32[]{:S(2)}) async-start(), calls=%async_computation.27 | async-start | bytes 2359296 | tf_op jit(solution)/shard_map/reduce_scatter | solution.py:283
  861.4 247.4 %reduce-scatter.19.cloned.1.call-start = ((), (), s32[]{:S(2)}) async-start(), calls=%async_computation.24 | async-start | bytes 2359296 | tf_op jit(solution)/shard_map/reduce_scatter | solution.py:274
  879.4 300.5 %reduce-scatter.23.cloned.1.call-start = ((), (), s32[]{:S(2)}) async-start(), calls=%async_computation.26 | async-start | bytes 2359296 | tf_op jit(solution)/shard_map/reduce_scatter | solution.py:280
  889.8 361.0 %reduce-scatter.21.cloned.1.call-start = ((), (), s32[]{:S(2)}) async-start(), calls=%async_computation.25 | async-start | bytes 2359296 | tf_op jit(solution)/shard_map/reduce_scatter | solution.py:277
  925.8 46.8 %copy-start.109 = (bf16[512,2048]{1,0:T(8,128)(2,1)S(1)}, bf16[512,2048]{1,0:T(8,128)(2,1)}, u32[]{:S(2)}) copy-start(bf16[512,2048]{1,0:T(8,128)(2,1)} %get-tuple-element.65) | copy-start | bytes 6291460
  972.4 433.5 %all-reduce.19.cloned.1.call-start = ((), (), s32[]{:S(2)}) async-start(), calls=%async_computation.30 | async-start | bytes 16777216 | tf_op jit(solution)/shard_map/psum | solution.py:172
  1002.5 14.4 copy-start.62
  1002.5 14.4 copy-start.77
  1002.5 556.0 %reduce-scatter.27.cloned.1.call-start = ((), (), s32[]{:S(2)}) async-start(), calls=%async_computation.28 | async-start | bytes 9437184 | tf_op jit(solution)/shard_map/reduce_scatter | solution.py:286
  1003.1 13.8 copy-start.6
  1032.6 676.5 %reduce-scatter.29.cloned.1.call-start = ((), (), s32[]{:S(2)}) async-start(), calls=%async_computation.29 | async-start | bytes 9437184 | tf_op jit(solution)/shard_map/reduce_scatter | solution.py:289
  1411.9 48.5 %copy-start.15 = (bf16[512,2048]{1,0:T(8,128)(2,1)S(1)}, bf16[512,2048]{1,0:T(8,128)(2,1)}, u32[]{:S(2)}) copy-start(bf16[512,2048]{1,0:T(8,128)(2,1)} %all-reduce.15.cloned.1.call-done) | copy-start | bytes 6291460
  1411.9 48.5 %copy-start.67 = (f32[2048]{0:T(1024)S(1)}, f32[2048]{0:T(1024)}, u32[]{:S(2)}) copy-start(f32[2048]{0:T(1024)} %param.40) | copy-start | bytes 24580
  1411.9 48.5 %copy-start.75 = (f32[512]{0:T(512)S(1)}, f32[512]{0:T(512)}, u32[]{:S(2)}) copy-start(f32[512]{0:T(512)} %copy-done.74) | copy-start | bytes 6148
  1411.9 48.5 %copy-start.91 = (f32[512]{0:T(512)S(1)}, f32[512]{0:T(512)}, u32[]{:S(2)}) copy-start(f32[512]{0:T(512)} %copy-done.90) | copy-start | bytes 6148
  (82 other events, 458.9 us)
Sparse Core Ops, SparseCore 0:
  9.5 35.8 all-gather.8
  46.9 33.0 all-gather.14
  81.6 33.0 all-gather.12
  116.7 45.6 all-gather.10
  163.8 31.8 all-gather.16
  200.1 51.3 all-reduce.14
  264.2 65.8 all-gather.22
  361.6 53.0 all-reduce.16
  416.3 104.0 all-gather.18
  521.8 103.9 all-gather.20
  672.2 85.4 all-reduce.20
  787.5 43.7 reduce-scatter.12
  833.6 42.8 reduce-scatter.16
  878.6 42.8 reduce-scatter.10
  923.6 42.8 reduce-scatter.14
  969.9 67.9 reduce-scatter.24
  1041.3 67.4 reduce-scatter.18
  1112.1 67.7 reduce-scatter.22
  1183.5 67.3 reduce-scatter.20
  1253.9 151.9 all-reduce.18
  1409.6 148.8 reduce-scatter.26
  1562.1 146.9 reduce-scatter.28
